TPU v7x, 256 devices: a whole 4x4x8 slice. The times are simulated.
256 devices in a mesh: tile: 128 (over z, x, y), sub: 2 (over core).
Axes of the slice: x: 4, y: 4, z: 8, core: 2. Of those that a mesh axis runs over, the one named last changes fastest.
Arguments:
- grid: bfloat16 [262144, 512], P(('tile', 'sub')), may hold values from -6 to 6
- g2m_owner: int32 [2048], P(('tile', 'sub')), may hold values from 0 to 255, as said below
- g2m_weight: float32 [262144], P(('tile', 'sub')), may hold values from 0.1 to 1
- m2g_owner: int32 [2048], P(('tile', 'sub')), may hold values from 0 to 255, as said below
- m2g_weight: float32 [262144], P(('tile', 'sub')), may hold values from 0.2 to 2
- mesh_feat: bfloat16 [32768, 512], P(('tile', 'sub')), may hold values from -6 to 6
- neighbours: int32 [256, 3], P(('tile', 'sub')), may hold values from 0 to 255, as said below
- enc_w1: bfloat16 [512, 2048], replicated, may hold values from -0.25 to 0.25
- enc_w2: bfloat16 [2048, 512], replicated, may hold values from -0.125 to 0.125
- attn_gain: float32 [1, 512], replicated, may hold values from 0.25 to 1.75
- w_qkv: bfloat16 [1, 512, 1536], replicated, may hold values from -1 to 1
- w_out: bfloat16 [1, 512, 512], replicated, may hold values from -0.25 to 0.25
- dec_w1: bfloat16 [512, 2048], replicated, may hold values from -0.25 to 0.25
- dec_w2: bfloat16 [2048, 512], replicated, may hold values from -0.125 to 0.125
Outputs:
- decoded: bfloat16 [262144, 512], P(('tile', 'sub'))
- mesh_out: bfloat16 [32768, 512], P(('tile', 'sub'))
Inputs may be any that keep to these rules, and one draw needn't show every extreme that they name: g2m_owner[b] equals b // 8 + e modulo 256 with e between -2 and 2; both -2 and 2 occur. m2g_owner[b] equals b // 8 + e modulo 256 with e between -2 and 2; both -2 and 2 occur. `neighbours`: row m holds three distinct blocks among m - 2, m - 1, m + 1, m + 2 modulo 256.
All inputs are finite; a program needn't handle non-finite values.
Results may differ from a plain program's by a relative error of at most 0.015.
Values may be sent and summed in bfloat16 or wider, within the bound.
A program may use at most 64 MiB of HBM per device.

v0:
```python
import functools

import jax
import jax.numpy as jnp
from jax import lax
from jax.experimental import pallas as pl
from jax.experimental.pallas import tpu as pltpu
from jax.sharding import PartitionSpec as P

HD = 128
DELTAS = (-2, 2, -1, 1)
SLOT = {-2: 0, -1: 1, 1: 2, 2: 3}
OWN = 4
CHUNKS = 4
LAG = 2
NEG = -1e30
BF = jnp.bfloat16
F32 = jnp.float32
NT = (((1,), (1,)), ((), ()))


def dot(a, b):
    return jnp.dot(a, b, preferred_element_type=F32)


def dot_nt(a, b):
    return lax.dot_general(a, b, NT, preferred_element_type=F32)


def hidden_layer(rows, w1, hid):
    width = 512
    for f in range(w1.shape[1] // width):
        cols = slice(f * width, (f + 1) * width)
        half = 0.5 * dot(rows, w1[:, cols])
        hid[:, cols] = (half + half * jnp.tanh(half)).astype(BF)


def step_kernel(
    grid_hbm, gown_hbm, gw_hbm, mown_hbm, mw_hbm, feat_hbm, neigh_hbm,
    ew1_hbm, ew2_hbm, gain_hbm, wqkv_hbm, wout_hbm, dw1_hbm, dw2_hbm,
    res, rin, mesh, dw1, dw2,
    x, enc, feat, state, nall, hid, qt, sown, bias, wvo, sel,
    ew1, ew2, wqkv, wout, gain, gw, mw, gwt, mwt,
    psend, precv, gown, mown, neigh, *rest,
):
    nc = CHUNKS
    cands = rest[:nc]
    lsem, s1, r1, s2, r2, s3, r3 = rest[nc:]
    nb, rows, depth = x.shape
    heads = depth // HD
    r = rows // nc
    m = nb * r
    count = lax.axis_size("tile") * lax.axis_size("sub")
    me = lax.axis_index("tile") * lax.axis_size("sub") + lax.axis_index("sub")

    def place(delta):
        d = lax.rem(me + delta + count, count)
        return (d // 2, lax.rem(d, 2))

    def offset(block):
        return lax.rem(block - me + 2 + count, count)

    barrier = pltpu.get_barrier_semaphore()
    for delta in DELTAS:
        pl.semaphore_signal(
            barrier, inc=1, device_id=place(delta), device_id_type=pl.DeviceIdType.MESH
        )

    loads = {}

    def load(name, src, dst):
        c = pltpu.make_async_copy(src, dst, lsem.at[len(loads)])
        c.start()
        loads[name] = c

    load("gown", gown_hbm, gown)
    load("gw", gw_hbm, gw)
    load("mown", mown_hbm, mown)
    load("mw", mw_hbm, mw)
    load("neigh", neigh_hbm, neigh)
    load("gain", gain_hbm, gain)
    load("x0", grid_hbm.at[:, 0:r, :], x.at[:, 0:r, :])
    load("ew1", ew1_hbm, ew1)
    load("ew2", ew2_hbm, ew2)
    for c in range(1, nc):
        load(f"x{c}", grid_hbm.at[:, c * r:(c + 1) * r, :], x.at[:, c * r:(c + 1) * r, :])
    load("feat", feat_hbm, feat)
    load("wqkv", wqkv_hbm.at[0], wqkv)
    load("wout", wout_hbm.at[0], wout)
    load("dw1", dw1_hbm, dw1)
    load("dw2", dw2_hbm, dw2)

    for name in ("gown", "gw", "mown", "mw", "neigh"):
        loads[name].wait()
    gwt[...] = jnp.tile(gw[...], (rows // nb, 1)).T
    mwt[...] = jnp.tile(mw[...], (rows // nb, 1)).T

    out_row = lax.broadcasted_iota(jnp.int32, (r, r), 0)
    in_row = lax.broadcasted_iota(jnp.int32, (r, r), 1)
    same = (out_row == in_row).astype(F32)
    for b in range(nb):
        e = offset(gown[b])
        for s in range(5):
            hit = jnp.where(e == s, 1.0, 0.0).astype(F32)
            sel[s * r:(s + 1) * r, b * r:(b + 1) * r] = (same * hit).astype(BF)
    for delta, s in SLOT.items():
        listed = jnp.int32(0)
        for j in range(3):
            listed = listed + jnp.where(offset(neigh[0, j]) == 2 + delta, 1, 0)
        fill = jnp.where(listed > 0, 0.0, NEG).astype(F32)
        bias[:, s * rows:(s + 1) * rows] = jnp.full((1, rows), fill, F32)

    def remote(src, dst, ssem, rsem, delta):
        return pltpu.make_async_remote_copy(
            src_ref=src, dst_ref=dst, send_sem=ssem, recv_sem=rsem,
            device_id=place(delta), device_id_type=pl.DeviceIdType.MESH,
        )

    sent = []
    first = {}
    second = {}
    third = {}

    def absorb(c):
        lo, hi = c * r, (c + 1) * r
        total = state[lo:hi, :]
        for k in range(len(DELTAS)):
            first[c, k].wait_recv()
            total = total + precv[c, k].astype(F32)
        state[lo:hi, :] = total
        mean_sq = jnp.mean(total * total, axis=-1, keepdims=True)
        nall[OWN, lo:hi, :] = (total * lax.rsqrt(mean_sq + 1e-06) * gain[...]).astype(BF)
        for k, delta in enumerate(DELTAS):
            copy = remote(
                nall.at[OWN, lo:hi, :], nall.at[SLOT[-delta], lo:hi, :],
                s2.at[c, k], r2.at[c, k], delta,
            )
            copy.start()
            second[c, k] = copy
            sent.append(copy)

    for c in range(nc):
        lo, hi = c * r, (c + 1) * r
        loads[f"x{c}"].wait()
        if c == 0:
            loads["ew1"].wait()
        xb = x[:, lo:hi, :].reshape(m, depth)
        hidden_layer(xb, ew1, hid)
        if c == 0:
            loads["ew2"].wait()
        wcol = jnp.concatenate([gwt[lo:hi, b:b + 1] for b in range(nb)], axis=0)
        y = xb.astype(F32) + dot(hid[...], ew2[...])
        enc[:, lo:hi, :] = y.astype(BF).reshape(nb, r, depth)
        part = dot(sel[...], (y * wcol).astype(BF))
        if c == 0:
            loads["feat"].wait()
            loads["gain"].wait()
            pl.semaphore_wait(barrier, len(DELTAS))
        state[lo:hi, :] = feat[lo:hi, :].astype(F32) + part[2 * r:3 * r]
        for k, delta in enumerate(DELTAS):
            psend[c, k] = part[(2 + delta) * r:(3 + delta) * r].astype(BF)
            copy = remote(psend.at[c, k], precv.at[c, k], s1.at[c, k], r1.at[c, k], delta)
            copy.start()
            first[c, k] = copy
            sent.append(copy)
        if c >= LAG:
            absorb(c - LAG)
    for c in range(nc - LAG, nc - 1):
        absorb(c)

    loads["wqkv"].wait()
    loads["wout"].wait()
    for h in range(heads):
        cols = slice(2 * depth + h * HD, 2 * depth + (h + 1) * HD)
        wvo[h * depth:(h + 1) * depth, :] = dot(
            wqkv[:, cols], wout[h * HD:(h + 1) * HD, :]
        ).astype(BF)
    absorb(nc - 1)

    parts = 2
    ar = rows // parts
    scale = HD ** -0.5
    q = dot(nall[OWN], wqkv[:, :depth]).astype(BF)
    for h in range(heads):
        t = scale * dot_nt(
            q[:, h * HD:(h + 1) * HD], wqkv[:, depth + h * HD:depth + (h + 1) * HD]
        )
        for p in range(parts):
            qt[p, h * ar:(h + 1) * ar, :] = t[p * ar:(p + 1) * ar].astype(BF)
    for p in range(parts):
        sown[p] = dot_nt(qt[p], nall[OWN])

    for c in range(nc):
        for k in range(len(DELTAS)):
            second[c, k].wait_recv()

    per = nc // parts
    for p in range(parts):
        scores = dot_nt(qt[p], nall[0:OWN].reshape(OWN * rows, depth)) + bias[...]
        scores = jnp.concatenate([scores, sown[p]], axis=1)
        top = jnp.max(scores, axis=-1, keepdims=True)
        e = jnp.exp(scores - top)
        total = jnp.sum(e, axis=-1, keepdims=True)
        mixed = dot(e.astype(BF), nall[...].reshape(5 * rows, depth))
        mixed = (mixed / total).astype(BF)
        mixed = jnp.concatenate([mixed[h * ar:(h + 1) * ar] for h in range(heads)], axis=1)
        new = (state[p * ar:(p + 1) * ar, :] + dot(mixed, wvo[...])).astype(BF)
        mesh[p * ar:(p + 1) * ar, :] = new
        for i in range(per):
            c = p * per + i
            cand = cands[c]
            cand[2] = new[i * r:(i + 1) * r]
            for k, delta in enumerate(DELTAS):
                copy = remote(
                    cand.at[2], cand.at[2 - delta], s3.at[c, k], r3.at[c, k], delta
                )
                copy.start()
                third[c, k] = copy
                sent.append(copy)

    loads["dw1"].wait()
    loads["dw2"].wait()
    for c in range(nc):
        lo, hi = c * r, (c + 1) * r
        for k in range(len(DELTAS)):
            third[c, k].wait_recv()
        pieces = []
        for b in range(nb):
            e = jnp.minimum(offset(mown[b]), 4)
            pieces.append(
                enc[b, lo:hi, :].astype(F32)
                + mwt[lo:hi, b:b + 1] * cands[c][e].astype(F32)
            )
        rows_in = jnp.concatenate(pieces, axis=0).astype(BF)
        if c == nc - 1:
            rin[...] = rows_in
            break
        hidden_layer(rows_in, dw1, hid)
        y = rows_in.astype(F32) + dot(hid[...], dw2[...])
        res[:, lo:hi, :] = y.astype(BF).reshape(nb, r, depth)
    for copy in sent:
        copy.wait_send()


def last_kernel(res, rin, mesh, dw1, dw2, dec_hbm, mesh_hbm, hid, tail, sem):
    nb, rows, depth = res.shape
    m = rin.shape[0]
    r = m // nb
    done = rows - r
    outs = [
        pltpu.make_async_copy(
            res.at[:, 0:done, :], dec_hbm.at[:, 0:done, :], sem.at[0]
        ),
        pltpu.make_async_copy(mesh, mesh_hbm, sem.at[1]),
    ]
    for out in outs:
        out.start()
    rows_in = rin[...]
    hidden_layer(rows_in, dw1, hid)
    y = rows_in.astype(F32) + dot(hid[...], dw2[...])
    tail[...] = y.astype(BF).reshape(nb, r, depth)
    out = pltpu.make_async_copy(tail, dec_hbm.at[:, done:, :], sem.at[2])
    out.start()
    outs.append(out)
    for out in outs:
        out.wait()


def on_device(
    grid, g2m_owner, g2m_weight, m2g_owner, m2g_weight, mesh_feat, neighbours,
    enc_w1, enc_w2, attn_gain, w_qkv, w_out, dec_w1, dec_w2,
):
    nb = g2m_owner.shape[0]
    rows, depth = mesh_feat.shape
    ff = enc_w1.shape[1]
    nc = CHUNKS
    r = rows // nc
    nd = len(DELTAS)
    heads = depth // HD
    any_spec = pl.BlockSpec(memory_space=pl.ANY)
    vm_spec = pl.BlockSpec(memory_space=pltpu.VMEM)
    dma = pltpu.SemaphoreType.DMA
    vm = pltpu.VMEM
    held = pl.pallas_call(
        step_kernel,
        out_shape=(
            vm((nb, rows, depth), BF),
            vm((nb * r, depth), BF),
            vm((rows, depth), BF),
            vm((depth, ff), BF),
            vm((ff, depth), BF),
        ),
        in_specs=[pl.BlockSpec(memory_space=pltpu.HBM)] * 14,
        out_specs=(vm_spec,) * 5,
        scratch_shapes=[
            vm((nb, rows, depth), BF),
            vm((nb, rows, depth), BF),
            vm((rows, depth), BF),
            vm((rows, depth), F32),
            vm((5, rows, depth), BF),
            vm((nb * r, ff), BF),
            vm((2, rows // 2 * heads, depth), BF),
            vm((2, rows // 2 * heads, rows), F32),
            vm((1, OWN * rows), F32),
            vm((heads * depth, depth), BF),
            vm((5 * r, nb * r), BF),
            vm((depth, ff), BF),
            vm((ff, depth), BF),
            vm((depth, 3 * depth), BF),
            vm((depth, depth), BF),
            vm((1, depth), F32),
            vm((nb, rows), F32),
            vm((nb, rows), F32),
            vm((rows, rows), F32),
            vm((rows, rows), F32),
            vm((nc, nd, r, depth), BF),
            vm((nc, nd, r, depth), BF),
            pltpu.SMEM((nb,), jnp.int32),
            pltpu.SMEM((nb,), jnp.int32),
            pltpu.SMEM((1, 3), jnp.int32),
        ]
        + [vm((5, r, depth), BF)] * nc
        + [dma((20,))]
        + [dma((nc, nd))] * 6,
        compiler_params=pltpu.CompilerParams(
            collective_id=0, has_side_effects=True, vmem_limit_bytes=40 * 2**20
        ),
        name="step",
    )(*[pltpu.with_memory_space_constraint(a, pltpu.HBM) for a in (
        grid.reshape(nb, rows, depth), g2m_owner, g2m_weight.reshape(nb, rows),
        m2g_owner, m2g_weight.reshape(nb, rows), mesh_feat, neighbours,
        enc_w1, enc_w2, attn_gain, w_qkv, w_out, dec_w1, dec_w2,
    )])
    decoded, mesh_out = pl.pallas_call(
        last_kernel,
        out_shape=(
            jax.ShapeDtypeStruct((nb, rows, depth), BF),
            jax.ShapeDtypeStruct((rows, depth), BF),
        ),
        in_specs=[vm_spec] * 5,
        out_specs=(any_spec, any_spec),
        scratch_shapes=[
            vm((nb * r, ff), BF),
            vm((nb, r, depth), BF),
            dma((3,)),
        ],
        compiler_params=pltpu.CompilerParams(vmem_limit_bytes=16 * 2**20),
        name="last",
    )(*[pltpu.with_memory_space_constraint(a, pltpu.VMEM) for a in held])
    return decoded.reshape(nb * rows, depth), mesh_out


def solution(mesh):
    cut = P(("tile", "sub"))
    cut2 = P(("tile", "sub"), None)
    in_specs = (cut2, cut, cut, cut, cut, cut2, cut2) + (P(),) * 7
    return jax.shard_map(
        on_device, mesh=mesh, in_specs=in_specs, out_specs=(cut2, cut2), check_vma=False
    )
```

profile of v0, /device:TPU:1, one launch (start us, length us, event | category | flops | bytes accessed | tf_op | source)
XLA Modules:
  0.0 45.4 jit_solution(17370595920350357538)
XLA Ops:
  0.6 42.6 %step.1 = (bf16[8,128,512]{2,1,0:T(8,128)(2,1)S(1)}, bf16[256,512]{1,0:T(8,128)(2,1)S(1)}, bf16[128,512]{1,0:T(8,128)(2,1)S(1)}, bf16[512,2048]{1,0:T(8,128)(2,1)S(1)}, bf16[2048,512]{1,0:T(8,128)(2,1)S(1)}) custom-call(bf16[8,128,512]{2,1,0:T(8,128)(2,1)} %bitcast.4, s32[8]{0:T(128)} %gown_hbm.1, f32[8,128]{1,0:T(8,128)} %bitcast.5, s32[8]{0:T(128)} %mown_hbm.1, ...), custom_call_target="tpu_custom_call" | custom-call | tf_op jit(solution)/shard_map/step/pallas_call | solution.py:284
  43.3 2.1 %last.1 = (bf16[8,128,512]{2,1,0:T(8,128)(2,1)}, bf16[128,512]{1,0:T(8,128)(2,1)}) custom-call(bf16[8,128,512]{2,1,0:T(8,128)(2,1)S(1)} %get-tuple-element.9.res, bf16[256,512]{1,0:T(8,128)(2,1)S(1)} %get-tuple-element.10.rin, bf16[128,512]{1,0:T(8,128)(2,1)S(1)} %get-tuple-element.11.mesh, bf16[512,2048]{1,0:T(8,128)(2,1)S(1)} %get-tuple-element.12.dw1, ...), custom_call_target="tpu_custom_call" | custom-call | tf_op jit(solution)/shard_map/last/pallas_call | solution.py:334
where the time goes:
time: 45.5 us; the launch traced here: 45.4 us
  Pallas kernels  44.8 us (98%)
  between operations  0.64 us (1%)
    pallas_call x1, Pallas kernels, on_device(): pl.pallas_call(step_kernel, out_shape=(vm((nb, rows, depth), BF), vm((nb...  42.6 us
    pallas_call x1, Pallas kernels, on_device(): pl.pallas_call(last_kernel, out_shape=(jax.ShapeDtypeStruct((nb, rows, de...  2.14 us

commit v1 on v0

--- a/solution.py
+++ b/solution.py
@@ -14,6 +14,13 @@
 CHUNKS = 4
 LAG = 2
 NEG = -1e30
+PLANE = 32
+EDGES = (
+    (0, (-2, -1), 1, -1),
+    (1, (-2,), -1, -2),
+    (PLANE - 2, (2,), 1, 2),
+    (PLANE - 1, (1, 2), -1, 1),
+)
 BF = jnp.bfloat16
 F32 = jnp.float32
 NT = (((1,), (1,)), ((), ()))
@@ -27,10 +34,11 @@
     return lax.dot_general(a, b, NT, preferred_element_type=F32)
 
 
-def hidden_layer(rows, w1, hid):
+def hidden_layer(rows, w1, hid, ready=lambda f: None):
     width = 512
-    for f in range(w1.shape[1] // width):
-        cols = slice(f * width, (f + 1) * width)
+    for f in range(0, w1.shape[1], width):
+        ready(f)
+        cols = slice(f, f + width)
         half = 0.5 * dot(rows, w1[:, cols])
         hid[:, cols] = (half + half * jnp.tanh(half)).astype(BF)
 
@@ -41,11 +49,11 @@
     res, rin, mesh, dw1, dw2,
     x, enc, feat, state, nall, hid, qt, sown, bias, wvo, sel,
     ew1, ew2, wqkv, wout, gain, gw, mw, gwt, mwt,
-    psend, precv, gown, mown, neigh, *rest,
+    psend, precv, wy, asend, arecv, xrecv, gown, mown, neigh, *rest,
 ):
     nc = CHUNKS
     cands = rest[:nc]
-    lsem, s1, r1, s2, r2, s3, r3 = rest[nc:]
+    lsem, s1, r1, s2, r2, s3, r3, sx, rx = rest[nc:]
     nb, rows, depth = x.shape
     heads = depth // HD
     r = rows // nc
@@ -80,7 +88,10 @@
     load("neigh", neigh_hbm, neigh)
     load("gain", gain_hbm, gain)
     load("x0", grid_hbm.at[:, 0:r, :], x.at[:, 0:r, :])
-    load("ew1", ew1_hbm, ew1)
+    width = 512
+    ff = ew1.shape[1]
+    for f in range(0, ff, width):
+        load(f"ew1_{f}", ew1_hbm.at[:, f:f + width], ew1.at[:, f:f + width])
     load("ew2", ew2_hbm, ew2)
     for c in range(1, nc):
         load(f"x{c}", grid_hbm.at[:, c * r:(c + 1) * r, :], x.at[:, c * r:(c + 1) * r, :])
@@ -116,55 +127,99 @@
             device_id=place(delta), device_id_type=pl.DeviceIdType.MESH,
         )
 
-    sent = []
-    first = {}
-    second = {}
-    third = {}
+    def spot(c):
+        return slice(c * r, (c + 1) * r)
+
+    def first(c, delta):
+        k = SLOT[delta]
+        return remote(psend.at[c, k], precv.at[c, k], s1.at[c, k], r1.at[c, k], delta)
+
+    def second(c, delta):
+        k = SLOT[delta]
+        return remote(
+            nall.at[OWN, spot(c), :], nall.at[SLOT[-delta], spot(c), :],
+            s2.at[c, k], r2.at[c, k], delta,
+        )
+
+    def across(c, delta):
+        k = SLOT[delta]
+        return remote(asend.at[c], arecv.at[c, k], s2.at[c, k], r2.at[c, k], delta)
+
+    def shared(c, partner, target):
+        return remote(psend.at[c, SLOT[target]], xrecv.at[c], sx.at[c], rx.at[c], partner)
+
+    def third(c, delta):
+        k = SLOT[delta]
+        cand = cands[c]
+        return remote(cand.at[2], cand.at[2 - delta], s3.at[c, k], r3.at[c, k], delta)
+
+    place_in_plane = lax.rem(me, PLANE)
+    inner = jnp.logical_and(place_in_plane > 1, place_in_plane < PLANE - 2)
+
+    def add(c, total, sources):
+        for source in sources:
+            first(c, -source).wait_recv()
+            total = total + precv[c, SLOT[-source]].astype(F32)
+        return total
+
+    def norm(total):
+        mean_sq = jnp.mean(total * total, axis=-1, keepdims=True)
+        return (total * lax.rsqrt(mean_sq + 1e-06) * gain[...]).astype(BF)
+
+    def finish(c, sources, targets):
+        total = add(c, state[spot(c), :], sources)
+        state[spot(c), :] = total
+        nall[OWN, spot(c), :] = norm(total)
+        for delta in targets:
+            second(c, delta).start()
+
+    def presum(c):
+        for q, cross, _, _ in EDGES:
+            @pl.when(place_in_plane == q)
+            def _(cross=cross):
+                total = add(c, state[spot(c), :], [d for d in DELTAS if d not in cross])
+                state[spot(c), :] = total
+                asend[c] = total.astype(BF)
+                for delta in cross:
+                    across(c, delta).start()
 
     def absorb(c):
-        lo, hi = c * r, (c + 1) * r
-        total = state[lo:hi, :]
-        for k in range(len(DELTAS)):
-            first[c, k].wait_recv()
-            total = total + precv[c, k].astype(F32)
-        state[lo:hi, :] = total
-        mean_sq = jnp.mean(total * total, axis=-1, keepdims=True)
-        nall[OWN, lo:hi, :] = (total * lax.rsqrt(mean_sq + 1e-06) * gain[...]).astype(BF)
-        for k, delta in enumerate(DELTAS):
-            copy = remote(
-                nall.at[OWN, lo:hi, :], nall.at[SLOT[-delta], lo:hi, :],
-                s2.at[c, k], r2.at[c, k], delta,
-            )
-            copy.start()
-            second[c, k] = copy
-            sent.append(copy)
-
-    for c in range(nc):
-        lo, hi = c * r, (c + 1) * r
-        loads[f"x{c}"].wait()
-        if c == 0:
-            loads["ew1"].wait()
-        xb = x[:, lo:hi, :].reshape(m, depth)
-        hidden_layer(xb, ew1, hid)
-        if c == 0:
-            loads["ew2"].wait()
-        wcol = jnp.concatenate([gwt[lo:hi, b:b + 1] for b in range(nb)], axis=0)
-        y = xb.astype(F32) + dot(hid[...], ew2[...])
-        enc[:, lo:hi, :] = y.astype(BF).reshape(nb, r, depth)
-        part = dot(sel[...], (y * wcol).astype(BF))
+        @pl.when(inner)
+        def _():
+            finish(c, DELTAS, DELTAS)
+
+        presum(c)
+
+    def contribute(c):
+        part = dot(sel[...], wy[...])
         if c == 0:
             loads["feat"].wait()
             loads["gain"].wait()
             pl.semaphore_wait(barrier, len(DELTAS))
-        state[lo:hi, :] = feat[lo:hi, :].astype(F32) + part[2 * r:3 * r]
-        for k, delta in enumerate(DELTAS):
-            psend[c, k] = part[(2 + delta) * r:(3 + delta) * r].astype(BF)
-            copy = remote(psend.at[c, k], precv.at[c, k], s1.at[c, k], r1.at[c, k], delta)
-            copy.start()
-            first[c, k] = copy
-            sent.append(copy)
+        state[spot(c), :] = feat[spot(c), :].astype(F32) + part[2 * r:3 * r]
+        for delta in DELTAS:
+            psend[c, SLOT[delta]] = part[(2 + delta) * r:(3 + delta) * r].astype(BF)
+            first(c, delta).start()
+        for q, _, partner, target in EDGES:
+            @pl.when(place_in_plane == q)
+            def _(partner=partner, target=target):
+                shared(c, partner, target).start()
+
+    for c in range(nc):
+        loads[f"x{c}"].wait()
+        xb = x[:, spot(c), :].reshape(m, depth)
+        hidden_layer(xb, ew1, hid, lambda f, c=c: c == 0 and loads[f"ew1_{f}"].wait())
+        if c > 0:
+            contribute(c - 1)
+        if c == 0:
+            loads["ew2"].wait()
+        wcol = jnp.concatenate([gwt[spot(c), b:b + 1] for b in range(nb)], axis=0)
+        y = xb.astype(F32) + dot(hid[...], ew2[...])
+        enc[:, spot(c), :] = y.astype(BF).reshape(nb, r, depth)
+        wy[...] = (y * wcol).astype(BF)
         if c >= LAG:
             absorb(c - LAG)
+    contribute(nc - 1)
     for c in range(nc - LAG, nc - 1):
         absorb(c)
 
@@ -176,6 +231,11 @@
             wqkv[:, cols], wout[h * HD:(h + 1) * HD, :]
         ).astype(BF)
     absorb(nc - 1)
+    for q, cross, _, _ in EDGES:
+        @pl.when(place_in_plane == q)
+        def _(cross=cross):
+            for c in range(nc):
+                finish(c, cross, [d for d in DELTAS if d not in cross])
 
     parts = 2
     ar = rows // parts
@@ -190,9 +250,27 @@
     for p in range(parts):
         sown[p] = dot_nt(qt[p], nall[OWN])
 
-    for c in range(nc):
-        for k in range(len(DELTAS)):
-            second[c, k].wait_recv()
+    @pl.when(inner)
+    def _():
+        for c in range(nc):
+            for delta in DELTAS:
+                second(c, delta).wait_recv()
+
+    for q, cross, partner, target in EDGES:
+        @pl.when(place_in_plane == q)
+        def _(cross=cross, partner=partner, target=target):
+            for c in range(nc):
+                for source in DELTAS:
+                    if source not in cross:
+                        second(c, -source).wait_recv()
+                shared(c, partner, target).wait_recv()
+                for source in cross:
+                    across(c, -source).wait_recv()
+                    total = arecv[c, SLOT[-source]].astype(F32)
+                    total = total + psend[c, SLOT[source]].astype(F32)
+                    if source == target:
+                        total = total + xrecv[c].astype(F32)
+                    nall[SLOT[source], spot(c), :] = norm(total)
 
     per = nc // parts
     for p in range(parts):
@@ -208,22 +286,16 @@
         mesh[p * ar:(p + 1) * ar, :] = new
         for i in range(per):
             c = p * per + i
-            cand = cands[c]
-            cand[2] = new[i * r:(i + 1) * r]
-            for k, delta in enumerate(DELTAS):
-                copy = remote(
-                    cand.at[2], cand.at[2 - delta], s3.at[c, k], r3.at[c, k], delta
-                )
-                copy.start()
-                third[c, k] = copy
-                sent.append(copy)
+            cands[c][2] = new[i * r:(i + 1) * r]
+            for delta in DELTAS:
+                third(c, delta).start()
 
     loads["dw1"].wait()
     loads["dw2"].wait()
     for c in range(nc):
         lo, hi = c * r, (c + 1) * r
-        for k in range(len(DELTAS)):
-            third[c, k].wait_recv()
+        for delta in DELTAS:
+            third(c, delta).wait_recv()
         pieces = []
         for b in range(nb):
             e = jnp.minimum(offset(mown[b]), 4)
@@ -238,8 +310,27 @@
         hidden_layer(rows_in, dw1, hid)
         y = rows_in.astype(F32) + dot(hid[...], dw2[...])
         res[:, lo:hi, :] = y.astype(BF).reshape(nb, r, depth)
-    for copy in sent:
-        copy.wait_send()
+    for c in range(nc):
+        for delta in DELTAS:
+            first(c, delta).wait_send()
+            third(c, delta).wait_send()
+
+    @pl.when(inner)
+    def _():
+        for c in range(nc):
+            for delta in DELTAS:
+                second(c, delta).wait_send()
+
+    for q, cross, partner, target in EDGES:
+        @pl.when(place_in_plane == q)
+        def _(cross=cross, partner=partner, target=target):
+            for c in range(nc):
+                shared(c, partner, target).wait_send()
+                for delta in DELTAS:
+                    if delta in cross:
+                        across(c, delta).wait_send()
+                    else:
+                        second(c, delta).wait_send()
 
 
 def last_kernel(res, rin, mesh, dw1, dw2, dec_hbm, mesh_hbm, hid, tail, sem):
@@ -315,13 +406,18 @@
             vm((rows, rows), F32),
             vm((nc, nd, r, depth), BF),
             vm((nc, nd, r, depth), BF),
+            vm((nb * r, depth), BF),
+            vm((nc, r, depth), BF),
+            vm((nc, nd, r, depth), BF),
+            vm((nc, r, depth), BF),
             pltpu.SMEM((nb,), jnp.int32),
             pltpu.SMEM((nb,), jnp.int32),
             pltpu.SMEM((1, 3), jnp.int32),
         ]
         + [vm((5, r, depth), BF)] * nc
-        + [dma((20,))]
-        + [dma((nc, nd))] * 6,
+        + [dma((24,))]
+        + [dma((nc, nd))] * 6
+        + [dma((nc,))] * 2,
         compiler_params=pltpu.CompilerParams(
             collective_id=0, has_side_effects=True, vmem_limit_bytes=40 * 2**20
         ),

time: 45.5 us -> 42.3 us (0.930)
  Pallas kernels: 44.8 us -> 41.4 us
    pallas_call x1, Pallas kernels: 42.6 us -> 39.3 us  [on_device(): pl.pallas_call(step_kernel, out_shape=(vm((nb, rows, depth), BF), vm((nb...]
where the time goes in v1:
time: 42.3 us; the launch traced here: 42.2 us
  Pallas kernels  41.4 us (98%)
  between operations  0.8 us (2%)
    pallas_call x1, Pallas kernels, on_device(): pl.pallas_call(step_kernel, out_shape=(vm((nb, rows, depth), BF), vm((nb...  39.3 us
    pallas_call x1, Pallas kernels, on_device(): pl.pallas_call(last_kernel, out_shape=(jax.ShapeDtypeStruct((nb, rows, de...  2.14 us

profile of v1, /device:TPU:1, one launch (start us, length us, event | category | flops | bytes accessed | tf_op | source)
XLA Modules:
  0.0 42.2 jit_solution(12898086302397127086)
XLA Ops:
  0.6 39.3 %step.1 = (bf16[8,128,512]{2,1,0:T(8,128)(2,1)S(1)}, bf16[256,512]{1,0:T(8,128)(2,1)S(1)}, bf16[128,512]{1,0:T(8,128)(2,1)S(1)}, bf16[512,2048]{1,0:T(8,128)(2,1)S(1)}, bf16[2048,512]{1,0:T(8,128)(2,1)S(1)}) custom-call(bf16[8,128,512]{2,1,0:T(8,128)(2,1)} %bitcast.4, s32[8]{0:T(128)} %gown_hbm.1, f32[8,128]{1,0:T(8,128)} %bitcast.5, s32[8]{0:T(128)} %mown_hbm.1, ...), custom_call_target="tpu_custom_call" | custom-call | tf_op jit(solution)/shard_map/step/pallas_call | solution.py:375
  39.9 2.1 %last.1 = (bf16[8,128,512]{2,1,0:T(8,128)(2,1)}, bf16[128,512]{1,0:T(8,128)(2,1)}) custom-call(bf16[8,128,512]{2,1,0:T(8,128)(2,1)S(1)} %get-tuple-element.9.res, bf16[256,512]{1,0:T(8,128)(2,1)S(1)} %get-tuple-element.10.rin, bf16[128,512]{1,0:T(8,128)(2,1)S(1)} %get-tuple-element.11.mesh, bf16[512,2048]{1,0:T(8,128)(2,1)S(1)} %get-tuple-element.12.dw1, ...), custom_call_target="tpu_custom_call" | custom-call | tf_op jit(solution)/shard_map/last/pallas_call | solution.py:430

commit v2 on v1

--- a/solution.py
+++ b/solution.py
@@ -34,6 +34,12 @@
     return lax.dot_general(a, b, NT, preferred_element_type=F32)
 
 
+def crosses_up(position, delta):
+    if delta < 0:
+        return jnp.bool_(False)
+    return jnp.logical_and(position < PLANE, position + delta >= PLANE)
+
+
 def hidden_layer(rows, w1, hid, ready=lambda f: None):
     width = 512
     for f in range(0, w1.shape[1], width):
@@ -53,7 +59,7 @@
 ):
     nc = CHUNKS
     cands = rest[:nc]
-    lsem, s1, r1, s2, r2, s3, r3, sx, rx = rest[nc:]
+    lsem, ssem, r1, r1x, r2, r2x, r3, rx, ready = rest[nc:]
     nb, rows, depth = x.shape
     heads = depth // HD
     r = rows // nc
@@ -68,11 +74,28 @@
     def offset(block):
         return lax.rem(block - me + 2 + count, count)
 
+    place_in_plane = lax.rem(me, PLANE)
+    inner = jnp.logical_and(place_in_plane > 1, place_in_plane < PLANE - 2)
+    first_plane = me < PLANE
+    last_plane = me >= count - PLANE
+
+    def tell(sem, delta):
+        pl.semaphore_signal(
+            sem, inc=1, device_id=place(delta), device_id_type=pl.DeviceIdType.MESH
+        )
+
     barrier = pltpu.get_barrier_semaphore()
     for delta in DELTAS:
-        pl.semaphore_signal(
-            barrier, inc=1, device_id=place(delta), device_id_type=pl.DeviceIdType.MESH
-        )
+        @pl.when(jnp.logical_not(crosses_up(place_in_plane, delta)))
+        def _(delta=delta):
+            tell(barrier, delta)
+
+    def enter(cross):
+        right = bool(cross) and cross[0] < 0
+        pl.semaphore_wait(barrier, len(DELTAS) - (len(cross) if right else 0))
+        if cross and not right:
+            for delta in cross:
+                tell(ready, delta)
 
     loads = {}
 
@@ -130,80 +153,127 @@
     def spot(c):
         return slice(c * r, (c + 1) * r)
 
-    def first(c, delta):
-        k = SLOT[delta]
-        return remote(psend.at[c, k], precv.at[c, k], s1.at[c, k], r1.at[c, k], delta)
-
-    def second(c, delta):
+    def first(c, delta, cross=()):
         k = SLOT[delta]
         return remote(
+            psend.at[c, k], precv.at[c, k], ssem.at[0],
+            (r1x if delta in cross else r1).at[c], delta,
+        )
+
+    def second(c, delta):
+        return remote(
             nall.at[OWN, spot(c), :], nall.at[SLOT[-delta], spot(c), :],
-            s2.at[c, k], r2.at[c, k], delta,
+            ssem.at[1], r2.at[0], delta,
         )
 
     def across(c, delta):
-        k = SLOT[delta]
-        return remote(asend.at[c], arecv.at[c, k], s2.at[c, k], r2.at[c, k], delta)
+        return remote(asend.at[c], arecv.at[c, SLOT[delta]], ssem.at[1], r2x.at[0], delta)
 
     def shared(c, partner, target):
-        return remote(psend.at[c, SLOT[target]], xrecv.at[c], sx.at[c], rx.at[c], partner)
+        return remote(psend.at[c, SLOT[target]], xrecv.at[c], ssem.at[2], rx.at[0], partner)
 
     def third(c, delta):
-        k = SLOT[delta]
         cand = cands[c]
-        return remote(cand.at[2], cand.at[2 - delta], s3.at[c, k], r3.at[c, k], delta)
-
-    place_in_plane = lax.rem(me, PLANE)
-    inner = jnp.logical_and(place_in_plane > 1, place_in_plane < PLANE - 2)
-
-    def add(c, total, sources):
-        for source in sources:
-            first(c, -source).wait_recv()
-            total = total + precv[c, SLOT[-source]].astype(F32)
-        return total
+        return remote(cand.at[2], cand.at[2 - delta], ssem.at[3], r3.at[c], delta)
+
+    def arrived(ref, sem):
+        remote(ref, ref, ssem.at[0], sem, 1).wait_recv()
+
+    def left(ref, sem):
+        remote(ref, ref, sem, r1.at[0], 1).wait_send()
+
+    def local(cross):
+        return [d for d in DELTAS if d not in cross]
 
     def norm(total):
         mean_sq = jnp.mean(total * total, axis=-1, keepdims=True)
         return (total * lax.rsqrt(mean_sq + 1e-06) * gain[...]).astype(BF)
 
-    def finish(c, sources, targets):
-        total = add(c, state[spot(c), :], sources)
+    def add(c, sources):
+        total = state[spot(c), :]
+        for source in sources:
+            total = total + precv[c, SLOT[-source]].astype(F32)
         state[spot(c), :] = total
+        return total
+
+    def finish(c, sources, targets, sem):
+        arrived(precv.at[c, 0:len(sources)], sem.at[c])
+        total = add(c, sources)
         nall[OWN, spot(c), :] = norm(total)
         for delta in targets:
             second(c, delta).start()
 
-    def presum(c):
-        for q, cross, _, _ in EDGES:
-            @pl.when(place_in_plane == q)
-            def _(cross=cross):
-                total = add(c, state[spot(c), :], [d for d in DELTAS if d not in cross])
-                state[spot(c), :] = total
-                asend[c] = total.astype(BF)
-                for delta in cross:
-                    across(c, delta).start()
-
-    def absorb(c):
+    def presum(c, cross):
+        here = local(cross)
+        arrived(precv.at[c, 0:len(here)], r1.at[c])
+        asend[c] = add(c, here).astype(BF)
+        for delta in cross:
+            across(c, delta).start()
+
+    def open_right(done, cross):
+        pl.semaphore_wait(ready, len(cross))
+        for c in range(done):
+            for delta in cross:
+                first(c, delta, cross).start()
+
+    def absorb(c, late=False):
         @pl.when(inner)
         def _():
-            finish(c, DELTAS, DELTAS)
-
-        presum(c)
+            finish(c, DELTAS, DELTAS, r1)
+
+        for q, cross, _, _ in EDGES:
+            right = cross[0] < 0
+            on = place_in_plane == q
+            if right and not late:
+                on = jnp.logical_and(on, jnp.logical_not(first_plane))
+
+            @pl.when(on)
+            def _(cross=cross):
+                presum(c, cross)
 
     def contribute(c):
         part = dot(sel[...], wy[...])
         if c == 0:
             loads["feat"].wait()
             loads["gain"].wait()
-            pl.semaphore_wait(barrier, len(DELTAS))
         state[spot(c), :] = feat[spot(c), :].astype(F32) + part[2 * r:3 * r]
         for delta in DELTAS:
             psend[c, SLOT[delta]] = part[(2 + delta) * r:(3 + delta) * r].astype(BF)
-            first(c, delta).start()
-        for q, _, partner, target in EDGES:
+
+        @pl.when(inner)
+        def _():
+            if c == 0:
+                enter(())
+            for delta in DELTAS:
+                first(c, delta).start()
+
+        for q, cross, partner, target in EDGES:
+            right = cross[0] < 0
+
             @pl.when(place_in_plane == q)
-            def _(partner=partner, target=target):
+            def _(cross=cross, partner=partner, target=target, right=right):
+                if c == 0:
+                    if right:
+                        enter(cross)
+                    else:
+                        pl.when(jnp.logical_not(last_plane))(lambda: enter(cross))
+                if not right:
+                    for delta in cross:
+                        first(c, delta, cross).start()
+                elif c >= LAG:
+                    @pl.when(jnp.logical_not(first_plane))
+                    def _():
+                        for delta in cross:
+                            first(c, delta, cross).start()
+                for delta in local(cross):
+                    first(c, delta, cross).start()
                 shared(c, partner, target).start()
+
+    for q, cross, _, _ in EDGES:
+        if cross[0] > 0:
+            @pl.when(jnp.logical_and(place_in_plane == q, last_plane))
+            def _(cross=cross):
+                enter(cross)
 
     for c in range(nc):
         loads[f"x{c}"].wait()
@@ -217,11 +287,25 @@
         y = xb.astype(F32) + dot(hid[...], ew2[...])
         enc[:, spot(c), :] = y.astype(BF).reshape(nb, r, depth)
         wy[...] = (y * wcol).astype(BF)
+        if c == LAG:
+            for q, cross, _, _ in EDGES:
+                if cross[0] < 0:
+                    @pl.when(jnp.logical_and(place_in_plane == q, jnp.logical_not(first_plane)))
+                    def _(cross=cross):
+                        open_right(LAG, cross)
+        if c == nc - 1:
+            contribute(c)
         if c >= LAG:
             absorb(c - LAG)
-    contribute(nc - 1)
+    for q, cross, _, _ in EDGES:
+        if cross[0] < 0:
+            @pl.when(jnp.logical_and(place_in_plane == q, first_plane))
+            def _(cross=cross):
+                open_right(nc, cross)
+                for c in range(nc - LAG):
+                    presum(c, cross)
     for c in range(nc - LAG, nc - 1):
-        absorb(c)
+        absorb(c, True)
 
     loads["wqkv"].wait()
     loads["wout"].wait()
@@ -230,12 +314,12 @@
         wvo[h * depth:(h + 1) * depth, :] = dot(
             wqkv[:, cols], wout[h * HD:(h + 1) * HD, :]
         ).astype(BF)
-    absorb(nc - 1)
+    absorb(nc - 1, True)
     for q, cross, _, _ in EDGES:
         @pl.when(place_in_plane == q)
         def _(cross=cross):
             for c in range(nc):
-                finish(c, cross, [d for d in DELTAS if d not in cross])
+                finish(c, cross, local(cross), r1x)
 
     parts = 2
     ar = rows // parts
@@ -252,20 +336,16 @@
 
     @pl.when(inner)
     def _():
-        for c in range(nc):
-            for delta in DELTAS:
-                second(c, delta).wait_recv()
+        arrived(nall.at[0:OWN], r2.at[0])
 
     for q, cross, partner, target in EDGES:
         @pl.when(place_in_plane == q)
-        def _(cross=cross, partner=partner, target=target):
+        def _(cross=cross, target=target):
+            arrived(nall.at[0:OWN - len(cross)], r2.at[0])
+            arrived(xrecv, rx.at[0])
+            arrived(arecv.at[:, 0:len(cross)], r2x.at[0])
             for c in range(nc):
-                for source in DELTAS:
-                    if source not in cross:
-                        second(c, -source).wait_recv()
-                shared(c, partner, target).wait_recv()
                 for source in cross:
-                    across(c, -source).wait_recv()
                     total = arecv[c, SLOT[-source]].astype(F32)
                     total = total + psend[c, SLOT[source]].astype(F32)
                     if source == target:
@@ -294,8 +374,7 @@
     loads["dw2"].wait()
     for c in range(nc):
         lo, hi = c * r, (c + 1) * r
-        for delta in DELTAS:
-            third(c, delta).wait_recv()
+        arrived(psend.at[c], r3.at[c])
         pieces = []
         for b in range(nb):
             e = jnp.minimum(offset(mown[b]), 4)
@@ -310,27 +389,12 @@
         hidden_layer(rows_in, dw1, hid)
         y = rows_in.astype(F32) + dot(hid[...], dw2[...])
         res[:, lo:hi, :] = y.astype(BF).reshape(nb, r, depth)
-    for c in range(nc):
-        for delta in DELTAS:
-            first(c, delta).wait_send()
-            third(c, delta).wait_send()
-
-    @pl.when(inner)
+    for i in (0, 1, 3):
+        left(psend, ssem.at[i])
+
+    @pl.when(jnp.logical_not(inner))
     def _():
-        for c in range(nc):
-            for delta in DELTAS:
-                second(c, delta).wait_send()
-
-    for q, cross, partner, target in EDGES:
-        @pl.when(place_in_plane == q)
-        def _(cross=cross, partner=partner, target=target):
-            for c in range(nc):
-                shared(c, partner, target).wait_send()
-                for delta in DELTAS:
-                    if delta in cross:
-                        across(c, delta).wait_send()
-                    else:
-                        second(c, delta).wait_send()
+        left(xrecv, ssem.at[2])
 
 
 def last_kernel(res, rin, mesh, dw1, dw2, dec_hbm, mesh_hbm, hid, tail, sem):
@@ -415,9 +479,9 @@
             pltpu.SMEM((1, 3), jnp.int32),
         ]
         + [vm((5, r, depth), BF)] * nc
-        + [dma((24,))]
-        + [dma((nc, nd))] * 6
-        + [dma((nc,))] * 2,
+        + [dma((22,))]
+        + [dma((4,)), dma((nc,)), dma((nc,)), dma((1,)), dma((1,)), dma((nc,)), dma((1,))]
+        + [pltpu.SemaphoreType.REGULAR],
         compiler_params=pltpu.CompilerParams(
             collective_id=0, has_side_effects=True, vmem_limit_bytes=40 * 2**20
         ),

time: 42.3 us -> 39.4 us (0.931)
  Pallas kernels: 41.4 us -> 38.5 us
    pallas_call x1, Pallas kernels: 39.3 us -> 36.4 us  [on_device(): pl.pallas_call(step_kernel, out_shape=(vm((nb, rows, depth), BF), vm((nb...]
where the time goes in v2:
time: 39.4 us; the launch traced here: 39.3 us
  Pallas kernels  38.5 us (98%)
  between operations  0.8 us (2%)
    pallas_call x1, Pallas kernels, on_device(): pl.pallas_call(step_kernel, out_shape=(vm((nb, rows, depth), BF), vm((nb...  36.4 us
    pallas_call x1, Pallas kernels, on_device(): pl.pallas_call(last_kernel, out_shape=(jax.ShapeDtypeStruct((nb, rows, de...  2.13 us

profile of v2, /device:TPU:1, one launch (start us, length us, event | category | flops | bytes accessed | tf_op | source)
XLA Modules:
  0.0 39.3 jit_solution(8006866569559385561)
XLA Ops:
  0.6 36.4 %step.1 = (bf16[8,128,512]{2,1,0:T(8,128)(2,1)S(1)}, bf16[256,512]{1,0:T(8,128)(2,1)S(1)}, bf16[128,512]{1,0:T(8,128)(2,1)S(1)}, bf16[512,2048]{1,0:T(8,128)(2,1)S(1)}, bf16[2048,512]{1,0:T(8,128)(2,1)S(1)}) custom-call(bf16[8,128,512]{2,1,0:T(8,128)(2,1)} %bitcast.4, s32[8]{0:T(128)} %gown_hbm.1, f32[8,128]{1,0:T(8,128)} %bitcast.5, s32[8]{0:T(128)} %mown_hbm.1, ...), custom_call_target="tpu_custom_call" | custom-call | tf_op jit(solution)/shard_map/step/pallas_call | solution.py:439
  37.0 2.1 %last.1 = (bf16[8,128,512]{2,1,0:T(8,128)(2,1)}, bf16[128,512]{1,0:T(8,128)(2,1)}) custom-call(bf16[8,128,512]{2,1,0:T(8,128)(2,1)S(1)} %get-tuple-element.9.res, bf16[256,512]{1,0:T(8,128)(2,1)S(1)} %get-tuple-element.10.rin, bf16[128,512]{1,0:T(8,128)(2,1)S(1)} %get-tuple-element.11.mesh, bf16[512,2048]{1,0:T(8,128)(2,1)S(1)} %get-tuple-element.12.dw1, ...), custom_call_target="tpu_custom_call" | custom-call | tf_op jit(solution)/shard_map/last/pallas_call | solution.py:494

commit v3 on v2

--- a/solution.py
+++ b/solution.py
@@ -12,7 +12,7 @@
 SLOT = {-2: 0, -1: 1, 1: 2, 2: 3}
 OWN = 4
 CHUNKS = 4
-LAG = 2
+LAG = 3
 NEG = -1e30
 PLANE = 32
 EDGES = (
@@ -52,10 +52,10 @@
 def step_kernel(
     grid_hbm, gown_hbm, gw_hbm, mown_hbm, mw_hbm, feat_hbm, neigh_hbm,
     ew1_hbm, ew2_hbm, gain_hbm, wqkv_hbm, wout_hbm, dw1_hbm, dw2_hbm,
-    res, rin, mesh, dw1, dw2,
-    x, enc, feat, state, nall, hid, qt, sown, bias, wvo, sel,
+    res, rin, mesh, hout, dw2,
+    x, enc, feat, state, nall, hid, dw1, qt, sown, bias, wvo, sel,
     ew1, ew2, wqkv, wout, gain, gw, mw, gwt, mwt,
-    psend, precv, wy, asend, arecv, xrecv, gown, mown, neigh, *rest,
+    psend, precv, csend, asend, arecv, xrecv, gown, mown, neigh, *rest,
 ):
     nc = CHUNKS
     cands = rest[:nc]
@@ -76,7 +76,6 @@
 
     place_in_plane = lax.rem(me, PLANE)
     inner = jnp.logical_and(place_in_plane > 1, place_in_plane < PLANE - 2)
-    first_plane = me < PLANE
     last_plane = me >= count - PLANE
 
     def tell(sem, delta):
@@ -104,6 +103,8 @@
         c.start()
         loads[name] = c
 
+    width = 512
+    ff = ew1.shape[1]
     load("gown", gown_hbm, gown)
     load("gw", gw_hbm, gw)
     load("mown", mown_hbm, mown)
@@ -111,18 +112,24 @@
     load("neigh", neigh_hbm, neigh)
     load("gain", gain_hbm, gain)
     load("x0", grid_hbm.at[:, 0:r, :], x.at[:, 0:r, :])
-    width = 512
-    ff = ew1.shape[1]
     for f in range(0, ff, width):
         load(f"ew1_{f}", ew1_hbm.at[:, f:f + width], ew1.at[:, f:f + width])
     load("ew2", ew2_hbm, ew2)
     for c in range(1, nc):
-        load(f"x{c}", grid_hbm.at[:, c * r:(c + 1) * r, :], x.at[:, c * r:(c + 1) * r, :])
+        load(
+            f"x{c}", grid_hbm.at[:, c * r:(c + 1) * r, :], x.at[:, c * r:(c + 1) * r, :]
+        )
     load("feat", feat_hbm, feat)
     load("wqkv", wqkv_hbm.at[0], wqkv)
     load("wout", wout_hbm.at[0], wout)
     load("dw1", dw1_hbm, dw1)
     load("dw2", dw2_hbm, dw2)
+
+    for q, cross, _, _ in EDGES:
+        if cross[0] > 0:
+            @pl.when(jnp.logical_and(place_in_plane == q, last_plane))
+            def _(cross=cross):
+                enter(cross)
 
     for name in ("gown", "gw", "mown", "mw", "neigh"):
         loads[name].wait()
@@ -170,7 +177,21 @@
         return remote(asend.at[c], arecv.at[c, SLOT[delta]], ssem.at[1], r2x.at[0], delta)
 
     def shared(c, partner, target):
-        return remote(psend.at[c, SLOT[target]], xrecv.at[c], ssem.at[2], rx.at[0], partner)
+        return remote(psend.at[c, SLOT[target]], xrecv.at[c], ssem.at[2], rx.at[c], partner)
+
+    def both(c, target):
+        k = SLOT[target]
+        return remote(csend.at[c], precv.at[c, k], ssem.at[0], r1x.at[c], target)
+
+    def cross_over(c, partner, target):
+        if abs(target) == 2:
+            arrived(xrecv.at[c], rx.at[c])
+            csend[c] = (
+                psend[c, SLOT[target]].astype(F32) + xrecv[c].astype(F32)
+            ).astype(BF)
+            both(c, target).start()
+        else:
+            first(c, 2 * target, (2 * target,)).start()
 
     def third(c, delta):
         cand = cands[c]
@@ -181,6 +202,9 @@
 
     def left(ref, sem):
         remote(ref, ref, sem, r1.at[0], 1).wait_send()
+
+    def far(cross):
+        return -2 if cross[0] < 0 else 2
 
     def local(cross):
         return [d for d in DELTAS if d not in cross]
@@ -210,32 +234,23 @@
         for delta in cross:
             across(c, delta).start()
 
-    def open_right(done, cross):
+    def open_right(done, cross, partner, target):
         pl.semaphore_wait(ready, len(cross))
         for c in range(done):
-            for delta in cross:
-                first(c, delta, cross).start()
+            cross_over(c, partner, target)
 
     def absorb(c, late=False):
         @pl.when(inner)
         def _():
             finish(c, DELTAS, DELTAS, r1)
 
-        for q, cross, _, _ in EDGES:
-            right = cross[0] < 0
-            on = place_in_plane == q
-            if right and not late:
-                on = jnp.logical_and(on, jnp.logical_not(first_plane))
-
-            @pl.when(on)
-            def _(cross=cross):
-                presum(c, cross)
-
-    def contribute(c):
-        part = dot(sel[...], wy[...])
-        if c == 0:
-            loads["feat"].wait()
-            loads["gain"].wait()
+        if late:
+            for q, cross, _, _ in EDGES:
+                @pl.when(place_in_plane == q)
+                def _(cross=cross):
+                    presum(c, cross)
+
+    def contribute(c, part):
         state[spot(c), :] = feat[spot(c), :].astype(F32) + part[2 * r:3 * r]
         for delta in DELTAS:
             psend[c, SLOT[delta]] = part[(2 + delta) * r:(3 + delta) * r].astype(BF)
@@ -252,58 +267,51 @@
 
             @pl.when(place_in_plane == q)
             def _(cross=cross, partner=partner, target=target, right=right):
-                if c == 0:
-                    if right:
-                        enter(cross)
-                    else:
-                        pl.when(jnp.logical_not(last_plane))(lambda: enter(cross))
-                if not right:
-                    for delta in cross:
-                        first(c, delta, cross).start()
-                elif c >= LAG:
-                    @pl.when(jnp.logical_not(first_plane))
-                    def _():
-                        for delta in cross:
-                            first(c, delta, cross).start()
+                if c == 0 and right:
+                    enter(cross)
                 for delta in local(cross):
                     first(c, delta, cross).start()
                 shared(c, partner, target).start()
-
+                if not right and 0 < c:
+                    cross_over(c - 1, partner, target)
+
+    def open_chunk(c, ready=lambda f: None):
+        hidden_layer(x[:, spot(c), :].reshape(m, depth), ew1, hid.at[c % 2], ready)
+
+    loads["x0"].wait()
+    open_chunk(0, lambda f: loads[f"ew1_{f}"].wait())
     for q, cross, _, _ in EDGES:
         if cross[0] > 0:
-            @pl.when(jnp.logical_and(place_in_plane == q, last_plane))
+            @pl.when(jnp.logical_and(place_in_plane == q, jnp.logical_not(last_plane)))
             def _(cross=cross):
                 enter(cross)
 
+    for name in ["ew2", "feat", "gain"] + [f"x{c}" for c in range(1, nc)]:
+        loads[name].wait()
     for c in range(nc):
-        loads[f"x{c}"].wait()
-        xb = x[:, spot(c), :].reshape(m, depth)
-        hidden_layer(xb, ew1, hid, lambda f, c=c: c == 0 and loads[f"ew1_{f}"].wait())
-        if c > 0:
-            contribute(c - 1)
-        if c == 0:
-            loads["ew2"].wait()
-        wcol = jnp.concatenate([gwt[spot(c), b:b + 1] for b in range(nb)], axis=0)
-        y = xb.astype(F32) + dot(hid[...], ew2[...])
-        enc[:, spot(c), :] = y.astype(BF).reshape(nb, r, depth)
-        wy[...] = (y * wcol).astype(BF)
-        if c == LAG:
-            for q, cross, _, _ in EDGES:
-                if cross[0] < 0:
-                    @pl.when(jnp.logical_and(place_in_plane == q, jnp.logical_not(first_plane)))
-                    def _(cross=cross):
-                        open_right(LAG, cross)
-        if c == nc - 1:
-            contribute(c)
+        for _ in range(1):
+            wcol = jnp.concatenate([gwt[spot(c), b:b + 1] for b in range(nb)], axis=0)
+            y = x[:, spot(c), :].reshape(m, depth).astype(F32) + dot(hid[c % 2], ew2[...])
+            enc[:, spot(c), :] = y.astype(BF).reshape(nb, r, depth)
+            wy = (y * wcol).astype(BF)
+            if c < nc - 1:
+                open_chunk(c + 1)
+            part = dot(sel[...], wy)
+        contribute(c, part)
         if c >= LAG:
             absorb(c - LAG)
-    for q, cross, _, _ in EDGES:
-        if cross[0] < 0:
-            @pl.when(jnp.logical_and(place_in_plane == q, first_plane))
-            def _(cross=cross):
-                open_right(nc, cross)
-                for c in range(nc - LAG):
-                    presum(c, cross)
+    for q, cross, partner, target in EDGES:
+        right = cross[0] < 0
+
+        @pl.when(place_in_plane == q)
+        def _(cross=cross, partner=partner, target=target, right=right):
+            if right:
+                open_right(nc, cross, partner, target)
+            else:
+                cross_over(nc - 1, partner, target)
+            for c in range(nc - LAG):
+                presum(c, cross)
+
     for c in range(nc - LAG, nc - 1):
         absorb(c, True)
 
@@ -319,7 +327,7 @@
         @pl.when(place_in_plane == q)
         def _(cross=cross):
             for c in range(nc):
-                finish(c, cross, local(cross), r1x)
+                finish(c, (far(cross),), local(cross), r1x)
 
     parts = 2
     ar = rows // parts
@@ -342,7 +350,9 @@
         @pl.when(place_in_plane == q)
         def _(cross=cross, target=target):
             arrived(nall.at[0:OWN - len(cross)], r2.at[0])
-            arrived(xrecv, rx.at[0])
+            if abs(target) == 1:
+                for c in range(nc):
+                    arrived(xrecv.at[c], rx.at[c])
             arrived(arecv.at[:, 0:len(cross)], r2x.at[0])
             for c in range(nc):
                 for source in cross:
@@ -372,32 +382,42 @@
 
     loads["dw1"].wait()
     loads["dw2"].wait()
-    for c in range(nc):
-        lo, hi = c * r, (c + 1) * r
+    def read(c):
         arrived(psend.at[c], r3.at[c])
         pieces = []
         for b in range(nb):
             e = jnp.minimum(offset(mown[b]), 4)
             pieces.append(
-                enc[b, lo:hi, :].astype(F32)
-                + mwt[lo:hi, b:b + 1] * cands[c][e].astype(F32)
+                enc[b, spot(c), :].astype(F32)
+                + mwt[spot(c), b:b + 1] * cands[c][e].astype(F32)
             )
-        rows_in = jnp.concatenate(pieces, axis=0).astype(BF)
-        if c == nc - 1:
-            rin[...] = rows_in
-            break
-        hidden_layer(rows_in, dw1, hid)
-        y = rows_in.astype(F32) + dot(hid[...], dw2[...])
-        res[:, lo:hi, :] = y.astype(BF).reshape(nb, r, depth)
-    for i in (0, 1, 3):
+        return jnp.concatenate(pieces, axis=0).astype(BF)
+
+    rows_in = read(0)
+    hidden_layer(rows_in, dw1, hid.at[0])
+    for c in range(nc - 1):
+        after = read(c + 1)
+        for _ in range(1):
+            y = rows_in.astype(F32) + dot(hid[c % 2], dw2[...])
+            res[:, spot(c), :] = y.astype(BF).reshape(nb, r, depth)
+            hidden_layer(after, dw1, hout if c == nc - 2 else hid.at[(c + 1) % 2])
+        rows_in = after
+    rin[...] = rows_in
+    for i in (1, 3):
         left(psend, ssem.at[i])
 
-    @pl.when(jnp.logical_not(inner))
+    @pl.when(inner)
     def _():
-        left(xrecv, ssem.at[2])
-
-
-def last_kernel(res, rin, mesh, dw1, dw2, dec_hbm, mesh_hbm, hid, tail, sem):
+        left(psend, ssem.at[0])
+
+    for q, cross, _, _ in EDGES:
+        @pl.when(place_in_plane == q)
+        def _(cross=cross):
+            left(psend.at[:, 0:len(local(cross)) + 1], ssem.at[0])
+            left(xrecv, ssem.at[2])
+
+
+def last_kernel(res, rin, mesh, hid, dw2, dec_hbm, mesh_hbm, tail, sem):
     nb, rows, depth = res.shape
     m = rin.shape[0]
     r = m // nb
@@ -410,9 +430,7 @@
     ]
     for out in outs:
         out.start()
-    rows_in = rin[...]
-    hidden_layer(rows_in, dw1, hid)
-    y = rows_in.astype(F32) + dot(hid[...], dw2[...])
+    y = rin[...].astype(F32) + dot(hid[...], dw2[...])
     tail[...] = y.astype(BF).reshape(nb, r, depth)
     out = pltpu.make_async_copy(tail, dec_hbm.at[:, done:, :], sem.at[2])
     out.start()
@@ -442,7 +460,7 @@
             vm((nb, rows, depth), BF),
             vm((nb * r, depth), BF),
             vm((rows, depth), BF),
-            vm((depth, ff), BF),
+            vm((nb * r, ff), BF),
             vm((ff, depth), BF),
         ),
         in_specs=[pl.BlockSpec(memory_space=pltpu.HBM)] * 14,
@@ -453,7 +471,8 @@
             vm((rows, depth), BF),
             vm((rows, depth), F32),
             vm((5, rows, depth), BF),
-            vm((nb * r, ff), BF),
+            vm((2, nb * r, ff), BF),
+            vm((depth, ff), BF),
             vm((2, rows // 2 * heads, depth), BF),
             vm((2, rows // 2 * heads, rows), F32),
             vm((1, OWN * rows), F32),
@@ -470,7 +489,7 @@
             vm((rows, rows), F32),
             vm((nc, nd, r, depth), BF),
             vm((nc, nd, r, depth), BF),
-            vm((nb * r, depth), BF),
+            vm((nc, r, depth), BF),
             vm((nc, r, depth), BF),
             vm((nc, nd, r, depth), BF),
             vm((nc, r, depth), BF),
@@ -480,7 +499,7 @@
         ]
         + [vm((5, r, depth), BF)] * nc
         + [dma((22,))]
-        + [dma((4,)), dma((nc,)), dma((nc,)), dma((1,)), dma((1,)), dma((nc,)), dma((1,))]
+        + [dma((4,)), dma((nc,)), dma((nc,)), dma((1,)), dma((1,)), dma((nc,)), dma((nc,))]
         + [pltpu.SemaphoreType.REGULAR],
         compiler_params=pltpu.CompilerParams(
             collective_id=0, has_side_effects=True, vmem_limit_bytes=40 * 2**20
@@ -500,7 +519,6 @@
         in_specs=[vm_spec] * 5,
         out_specs=(any_spec, any_spec),
         scratch_shapes=[
-            vm((nb * r, ff), BF),
             vm((nb, r, depth), BF),
             dma((3,)),
         ],

time: 39.4 us -> 38 us (0.964)
  Pallas kernels: 38.5 us -> 37.1 us
    pallas_call x1, Pallas kernels: 36.4 us -> 35.7 us  [on_device(): pl.pallas_call(step_kernel, out_shape=(vm((nb, rows, depth), BF), vm((nb...]
    pallas_call x1, Pallas kernels: 2.13 us -> 1.44 us  [on_device(): pl.pallas_call(last_kernel, out_shape=(jax.ShapeDtypeStruct((nb, rows, de...]
where the time goes in v3:
time: 38 us; the launch traced here: 37.9 us
  Pallas kernels  37.1 us (98%)
  between operations  0.8 us (2%)
    pallas_call x1, Pallas kernels, on_device(): pl.pallas_call(step_kernel, out_shape=(vm((nb, rows, depth), BF), vm((nb...  35.7 us
    pallas_call x1, Pallas kernels, on_device(): pl.pallas_call(last_kernel, out_shape=(jax.ShapeDtypeStruct((nb, rows, de...  1.44 us

profile of v3, /device:TPU:1, one launch (start us, length us, event | category | flops | bytes accessed | tf_op | source)
XLA Modules:
  0.0 37.9 jit_solution(501716403392165591)
XLA Ops:
  0.6 35.7 %step.1 = (bf16[8,128,512]{2,1,0:T(8,128)(2,1)S(1)}, bf16[256,512]{1,0:T(8,128)(2,1)S(1)}, bf16[128,512]{1,0:T(8,128)(2,1)S(1)}, bf16[256,2048]{1,0:T(8,128)(2,1)S(1)}, bf16[2048,512]{1,0:T(8,128)(2,1)S(1)}) custom-call(bf16[8,128,512]{2,1,0:T(8,128)(2,1)} %bitcast.4, s32[8]{0:T(128)} %gown_hbm.1, f32[8,128]{1,0:T(8,128)} %bitcast.5, s32[8]{0:T(128)} %mown_hbm.1, ...), custom_call_target="tpu_custom_call" | custom-call | tf_op jit(solution)/shard_map/step/pallas_call | solution.py:457
  36.3 1.4 %last.1 = (bf16[8,128,512]{2,1,0:T(8,128)(2,1)}, bf16[128,512]{1,0:T(8,128)(2,1)}) custom-call(bf16[8,128,512]{2,1,0:T(8,128)(2,1)S(1)} %get-tuple-element.9.res, bf16[256,512]{1,0:T(8,128)(2,1)S(1)} %get-tuple-element.10.rin, bf16[128,512]{1,0:T(8,128)(2,1)S(1)} %get-tuple-element.11.mesh, bf16[256,2048]{1,0:T(8,128)(2,1)S(1)} %get-tuple-element.12.hid, ...), custom_call_target="tpu_custom_call" | custom-call | tf_op jit(solution)/shard_map/last/pallas_call | solution.py:513

commit v4 on v3

--- a/solution.py
+++ b/solution.py
@@ -15,6 +15,12 @@
 LAG = 3
 NEG = -1e30
 PLANE = 32
+SUMS = {
+    0: (-1, (-2,), None, -1),
+    1: (-2, (-2,), -2, None),
+    PLANE - 2: (2, (), None, 2),
+    PLANE - 1: (2, (1, 2), 1, None),
+}
 EDGES = (
     (0, (-2, -1), 1, -1),
     (1, (-2,), -1, -2),
@@ -40,10 +46,9 @@
     return jnp.logical_and(position < PLANE, position + delta >= PLANE)
 
 
-def hidden_layer(rows, w1, hid, ready=lambda f: None):
+def hidden_layer(rows, w1, hid):
     width = 512
     for f in range(0, w1.shape[1], width):
-        ready(f)
         cols = slice(f, f + width)
         half = 0.5 * dot(rows, w1[:, cols])
         hid[:, cols] = (half + half * jnp.tanh(half)).astype(BF)
@@ -59,7 +64,7 @@
 ):
     nc = CHUNKS
     cands = rest[:nc]
-    lsem, ssem, r1, r1x, r2, r2x, r3, rx, ready = rest[nc:]
+    lsem, ssem, r1, r1x, r2, r2x, r2f, r3, rx, ready = rest[nc:]
     nb, rows, depth = x.shape
     heads = depth // HD
     r = rows // nc
@@ -103,8 +108,6 @@
         c.start()
         loads[name] = c
 
-    width = 512
-    ff = ew1.shape[1]
     load("gown", gown_hbm, gown)
     load("gw", gw_hbm, gw)
     load("mown", mown_hbm, mown)
@@ -112,8 +115,8 @@
     load("neigh", neigh_hbm, neigh)
     load("gain", gain_hbm, gain)
     load("x0", grid_hbm.at[:, 0:r, :], x.at[:, 0:r, :])
-    for f in range(0, ff, width):
-        load(f"ew1_{f}", ew1_hbm.at[:, f:f + width], ew1.at[:, f:f + width])
+    for k in range(0, depth, HD):
+        load(f"ew1_{k}", ew1_hbm.at[k:k + HD, :], ew1.at[k:k + HD, :])
     load("ew2", ew2_hbm, ew2)
     for c in range(1, nc):
         load(
@@ -176,6 +179,10 @@
     def across(c, delta):
         return remote(asend.at[c], arecv.at[c, SLOT[delta]], ssem.at[1], r2x.at[0], delta)
 
+    def passed(c, partner, source):
+        own, other = SLOT[-source], SLOT[partner - source]
+        return remote(arecv.at[c, own], arecv.at[c, other], ssem.at[2], r2f.at[0], partner)
+
     def shared(c, partner, target):
         return remote(psend.at[c, SLOT[target]], xrecv.at[c], ssem.at[2], rx.at[c], partner)
 
@@ -227,12 +234,11 @@
         for delta in targets:
             second(c, delta).start()
 
-    def presum(c, cross):
+    def presum(c, cross, q):
         here = local(cross)
         arrived(precv.at[c, 0:len(here)], r1.at[c])
         asend[c] = add(c, here).astype(BF)
-        for delta in cross:
-            across(c, delta).start()
+        across(c, SUMS[q][0]).start()
 
     def open_right(done, cross, partner, target):
         pl.semaphore_wait(ready, len(cross))
@@ -247,8 +253,8 @@
         if late:
             for q, cross, _, _ in EDGES:
                 @pl.when(place_in_plane == q)
-                def _(cross=cross):
-                    presum(c, cross)
+                def _(cross=cross, q=q):
+                    presum(c, cross, q)
 
     def contribute(c, part):
         state[spot(c), :] = feat[spot(c), :].astype(F32) + part[2 * r:3 * r]
@@ -272,14 +278,18 @@
                 for delta in local(cross):
                     first(c, delta, cross).start()
                 shared(c, partner, target).start()
-                if not right and 0 < c:
+                if not right and len(cross) == 2:
+                    cross_over(c, partner, target)
+                if not right and len(cross) == 1 and c > 0:
                     cross_over(c - 1, partner, target)
 
-    def open_chunk(c, ready=lambda f: None):
-        hidden_layer(x[:, spot(c), :].reshape(m, depth), ew1, hid.at[c % 2], ready)
+    def open_chunk(c):
+        hidden_layer(x[:, spot(c), :].reshape(m, depth), ew1, hid.at[c % 2])
 
     loads["x0"].wait()
-    open_chunk(0, lambda f: loads[f"ew1_{f}"].wait())
+    for k in range(0, depth, HD):
+        loads[f"ew1_{k}"].wait()
+    open_chunk(0)
     for q, cross, _, _ in EDGES:
         if cross[0] > 0:
             @pl.when(jnp.logical_and(place_in_plane == q, jnp.logical_not(last_plane)))
@@ -304,13 +314,13 @@
         right = cross[0] < 0
 
         @pl.when(place_in_plane == q)
-        def _(cross=cross, partner=partner, target=target, right=right):
+        def _(cross=cross, partner=partner, target=target, right=right, q=q):
             if right:
                 open_right(nc, cross, partner, target)
-            else:
+            elif len(cross) == 1:
                 cross_over(nc - 1, partner, target)
             for c in range(nc - LAG):
-                presum(c, cross)
+                presum(c, cross, q)
 
     for c in range(nc - LAG, nc - 1):
         absorb(c, True)
@@ -348,12 +358,19 @@
 
     for q, cross, partner, target in EDGES:
         @pl.when(place_in_plane == q)
-        def _(cross=cross, target=target):
+        def _(cross=cross, partner=partner, target=target, q=q):
+            _, direct, onward, handed = SUMS[q]
+            if direct:
+                arrived(arecv.at[:, 0:len(direct)], r2x.at[0])
+            if onward is not None:
+                for c in range(nc):
+                    passed(c, partner, onward).start()
             arrived(nall.at[0:OWN - len(cross)], r2.at[0])
-            if abs(target) == 1:
+            if handed is not None:
+                arrived(arecv.at[:, 0:1], r2f.at[0])
+            if len(cross) == 2:
                 for c in range(nc):
                     arrived(xrecv.at[c], rx.at[c])
-            arrived(arecv.at[:, 0:len(cross)], r2x.at[0])
             for c in range(nc):
                 for source in cross:
                     total = arecv[c, SLOT[-source]].astype(F32)
@@ -403,18 +420,19 @@
             hidden_layer(after, dw1, hout if c == nc - 2 else hid.at[(c + 1) % 2])
         rows_in = after
     rin[...] = rows_in
-    for i in (1, 3):
-        left(psend, ssem.at[i])
+    left(psend, ssem.at[3])
 
     @pl.when(inner)
     def _():
-        left(psend, ssem.at[0])
+        for i in (0, 1):
+            left(psend, ssem.at[i])
 
     for q, cross, _, _ in EDGES:
         @pl.when(place_in_plane == q)
-        def _(cross=cross):
-            left(psend.at[:, 0:len(local(cross)) + 1], ssem.at[0])
-            left(xrecv, ssem.at[2])
+        def _(cross=cross, q=q):
+            for i in (0, 1):
+                left(psend.at[:, 0:len(local(cross)) + 1], ssem.at[i])
+            left(arecv.at[:, 0:1 if SUMS[q][2] is None else 2], ssem.at[2])
 
 
 def last_kernel(res, rin, mesh, hid, dw2, dec_hbm, mesh_hbm, tail, sem):
@@ -499,7 +517,7 @@
         ]
         + [vm((5, r, depth), BF)] * nc
         + [dma((22,))]
-        + [dma((4,)), dma((nc,)), dma((nc,)), dma((1,)), dma((1,)), dma((nc,)), dma((nc,))]
+        + [dma((4,)), dma((nc,)), dma((nc,)), dma((1,)), dma((1,)), dma((1,)), dma((nc,)), dma((nc,))]
         + [pltpu.SemaphoreType.REGULAR],
         compiler_params=pltpu.CompilerParams(
             collective_id=0, has_side_effects=True, vmem_limit_bytes=40 * 2**20

time: 38 us -> 37.6 us (0.989)
  no operation moved by 1% of the time
where the time goes in v4:
time: 37.6 us
  Pallas kernels  36.8 us (98%)
  between operations  0.8 us (2%)
    pallas_call x1, Pallas kernels, on_device(): pl.pallas_call(step_kernel, out_shape=(vm((nb, rows, depth), BF), vm((nb...  35.3 us
    pallas_call x1, Pallas kernels, on_device(): pl.pallas_call(last_kernel, out_shape=(jax.ShapeDtypeStruct((nb, rows, de...  1.44 us

profile of v4, /device:TPU:1, one launch (start us, length us, event | category | flops | bytes accessed | tf_op | source)
XLA Modules:
  0.0 37.6 jit_solution(16594837668068830676)
XLA Ops:
  0.6 35.3 %step.1 = (bf16[8,128,512]{2,1,0:T(8,128)(2,1)S(1)}, bf16[256,512]{1,0:T(8,128)(2,1)S(1)}, bf16[128,512]{1,0:T(8,128)(2,1)S(1)}, bf16[256,2048]{1,0:T(8,128)(2,1)S(1)}, bf16[2048,512]{1,0:T(8,128)(2,1)S(1)}) custom-call(bf16[8,128,512]{2,1,0:T(8,128)(2,1)} %bitcast.4, s32[8]{0:T(128)} %gown_hbm.1, f32[8,128]{1,0:T(8,128)} %bitcast.5, s32[8]{0:T(128)} %mown_hbm.1, ...), custom_call_target="tpu_custom_call" | custom-call | tf_op jit(solution)/shard_map/step/pallas_call | solution.py:475
  36.0 1.4 %last.1 = (bf16[8,128,512]{2,1,0:T(8,128)(2,1)}, bf16[128,512]{1,0:T(8,128)(2,1)}) custom-call(bf16[8,128,512]{2,1,0:T(8,128)(2,1)S(1)} %get-tuple-element.9.res, bf16[256,512]{1,0:T(8,128)(2,1)S(1)} %get-tuple-element.10.rin, bf16[128,512]{1,0:T(8,128)(2,1)S(1)} %get-tuple-element.11.mesh, bf16[256,2048]{1,0:T(8,128)(2,1)S(1)} %get-tuple-element.12.hid, ...), custom_call_target="tpu_custom_call" | custom-call | tf_op jit(solution)/shard_map/last/pallas_call | solution.py:531

commit v5 on v4

--- a/solution.py
+++ b/solution.py
@@ -115,18 +115,10 @@
     load("neigh", neigh_hbm, neigh)
     load("gain", gain_hbm, gain)
     load("x0", grid_hbm.at[:, 0:r, :], x.at[:, 0:r, :])
-    for k in range(0, depth, HD):
-        load(f"ew1_{k}", ew1_hbm.at[k:k + HD, :], ew1.at[k:k + HD, :])
+    load("ew1", ew1_hbm, ew1)
     load("ew2", ew2_hbm, ew2)
-    for c in range(1, nc):
-        load(
-            f"x{c}", grid_hbm.at[:, c * r:(c + 1) * r, :], x.at[:, c * r:(c + 1) * r, :]
-        )
+    load("x1", grid_hbm.at[:, r:rows, :], x.at[:, r:rows, :])
     load("feat", feat_hbm, feat)
-    load("wqkv", wqkv_hbm.at[0], wqkv)
-    load("wout", wout_hbm.at[0], wout)
-    load("dw1", dw1_hbm, dw1)
-    load("dw2", dw2_hbm, dw2)
 
     for q, cross, _, _ in EDGES:
         if cross[0] > 0:
@@ -287,8 +279,11 @@
         hidden_layer(x[:, spot(c), :].reshape(m, depth), ew1, hid.at[c % 2])
 
     loads["x0"].wait()
-    for k in range(0, depth, HD):
-        loads[f"ew1_{k}"].wait()
+    loads["ew1"].wait()
+    load("wqkv", wqkv_hbm.at[0], wqkv)
+    load("wout", wout_hbm.at[0], wout)
+    load("dw1", dw1_hbm, dw1)
+    load("dw2", dw2_hbm, dw2)
     open_chunk(0)
     for q, cross, _, _ in EDGES:
         if cross[0] > 0:
@@ -296,7 +291,7 @@
             def _(cross=cross):
                 enter(cross)
 
-    for name in ["ew2", "feat", "gain"] + [f"x{c}" for c in range(1, nc)]:
+    for name in ("ew2", "feat", "gain", "x1"):
         loads[name].wait()
     for c in range(nc):
         for _ in range(1):
@@ -365,19 +360,24 @@
             if onward is not None:
                 for c in range(nc):
                     passed(c, partner, onward).start()
-            arrived(nall.at[0:OWN - len(cross)], r2.at[0])
-            if handed is not None:
-                arrived(arecv.at[:, 0:1], r2f.at[0])
             if len(cross) == 2:
                 for c in range(nc):
                     arrived(xrecv.at[c], rx.at[c])
-            for c in range(nc):
-                for source in cross:
+
+            def complete(source):
+                for c in range(nc):
                     total = arecv[c, SLOT[-source]].astype(F32)
                     total = total + psend[c, SLOT[source]].astype(F32)
                     if source == target:
                         total = total + xrecv[c].astype(F32)
                     nall[SLOT[source], spot(c), :] = norm(total)
+
+            for source in direct:
+                complete(source)
+            arrived(nall.at[0:OWN - len(cross)], r2.at[0])
+            if handed is not None:
+                arrived(arecv.at[:, 0:1], r2f.at[0])
+                complete(handed)
 
     per = nc // parts
     for p in range(parts):
@@ -516,7 +516,7 @@
             pltpu.SMEM((1, 3), jnp.int32),
         ]
         + [vm((5, r, depth), BF)] * nc
-        + [dma((22,))]
+        + [dma((15,))]
         + [dma((4,)), dma((nc,)), dma((nc,)), dma((1,)), dma((1,)), dma((1,)), dma((nc,)), dma((nc,))]
         + [pltpu.SemaphoreType.REGULAR],
         compiler_params=pltpu.CompilerParams(

time: 37.6 us -> 37.6 us (level)
  no operation moved by 1% of the time
where the time goes in v5:
time: 37.6 us; the launch traced here: 37.5 us
  Pallas kernels  36.7 us (98%)
  between operations  0.8 us (2%)
    pallas_call x1, Pallas kernels, on_device(): pl.pallas_call(step_kernel, out_shape=(vm((nb, rows, depth), BF), vm((nb...  35.3 us
    pallas_call x1, Pallas kernels, on_device(): pl.pallas_call(last_kernel, out_shape=(jax.ShapeDtypeStruct((nb, rows, de...  1.44 us

profile of v5, /device:TPU:1, one launch (start us, length us, event | category | flops | bytes accessed | tf_op | source)
XLA Modules:
  0.0 37.5 jit_solution(17195417535263410290)
XLA Ops:
  0.6 35.3 %step.1 = (bf16[8,128,512]{2,1,0:T(8,128)(2,1)S(1)}, bf16[256,512]{1,0:T(8,128)(2,1)S(1)}, bf16[128,512]{1,0:T(8,128)(2,1)S(1)}, bf16[256,2048]{1,0:T(8,128)(2,1)S(1)}, bf16[2048,512]{1,0:T(8,128)(2,1)S(1)}) custom-call(bf16[8,128,512]{2,1,0:T(8,128)(2,1)} %bitcast.4, s32[8]{0:T(128)} %gown_hbm.1, f32[8,128]{1,0:T(8,128)} %bitcast.5, s32[8]{0:T(128)} %mown_hbm.1, ...), custom_call_target="tpu_custom_call" | custom-call | tf_op jit(solution)/shard_map/step/pallas_call | solution.py:475
  35.9 1.4 %last.1 = (bf16[8,128,512]{2,1,0:T(8,128)(2,1)}, bf16[128,512]{1,0:T(8,128)(2,1)}) custom-call(bf16[8,128,512]{2,1,0:T(8,128)(2,1)S(1)} %get-tuple-element.9.res, bf16[256,512]{1,0:T(8,128)(2,1)S(1)} %get-tuple-element.10.rin, bf16[128,512]{1,0:T(8,128)(2,1)S(1)} %get-tuple-element.11.mesh, bf16[256,2048]{1,0:T(8,128)(2,1)S(1)} %get-tuple-element.12.hid, ...), custom_call_target="tpu_custom_call" | custom-call | tf_op jit(solution)/shard_map/last/pallas_call | solution.py:531

commit v6 on v5

--- a/solution.py
+++ b/solution.py
@@ -448,11 +448,16 @@
     ]
     for out in outs:
         out.start()
-    y = rin[...].astype(F32) + dot(hid[...], dw2[...])
-    tail[...] = y.astype(BF).reshape(nb, r, depth)
-    out = pltpu.make_async_copy(tail, dec_hbm.at[:, done:, :], sem.at[2])
-    out.start()
-    outs.append(out)
+    half = dw2.shape[1] // 2
+    for i in range(2):
+        cols = slice(i * half, (i + 1) * half)
+        y = rin[:, cols].astype(F32) + dot(hid[...], dw2[:, cols])
+        tail[:, :, cols] = y.astype(BF).reshape(nb, r, half)
+        out = pltpu.make_async_copy(
+            tail.at[:, :, cols], dec_hbm.at[:, done:, cols], sem.at[2 + i]
+        )
+        out.start()
+        outs.append(out)
     for out in outs:
         out.wait()
 
@@ -538,7 +543,7 @@
         out_specs=(any_spec, any_spec),
         scratch_shapes=[
             vm((nb, r, depth), BF),
-            dma((3,)),
+            dma((4,)),
         ],
         compiler_params=pltpu.CompilerParams(vmem_limit_bytes=16 * 2**20),
         name="last",

time: 37.6 us -> 38.2 us (1.016)
  Pallas kernels: 36.7 us -> 37.3 us
    pallas_call x1, Pallas kernels: 1.44 us -> 2.07 us  [on_device(): pl.pallas_call(last_kernel, out_shape=(jax.ShapeDtypeStruct((nb, rows, de...]
where the time goes in v6:
time: 38.2 us; the launch traced here: 38.1 us
  Pallas kernels  37.3 us (98%)
  between operations  0.8 us (2%)
    pallas_call x1, Pallas kernels, on_device(): pl.pallas_call(step_kernel, out_shape=(vm((nb, rows, depth), BF), vm((nb...  35.3 us
    pallas_call x1, Pallas kernels, on_device(): pl.pallas_call(last_kernel, out_shape=(jax.ShapeDtypeStruct((nb, rows, de...  2.07 us

profile of v6, /device:TPU:1, one launch (start us, length us, event | category | flops | bytes accessed | tf_op | source)
XLA Modules:
  0.0 38.1 jit_solution(7539285263855262816)
XLA Ops:
  0.6 35.3 %step.1 = (bf16[8,128,512]{2,1,0:T(8,128)(2,1)S(1)}, bf16[256,512]{1,0:T(8,128)(2,1)S(1)}, bf16[128,512]{1,0:T(8,128)(2,1)S(1)}, bf16[256,2048]{1,0:T(8,128)(2,1)S(1)}, bf16[2048,512]{1,0:T(8,128)(2,1)S(1)}) custom-call(bf16[8,128,512]{2,1,0:T(8,128)(2,1)} %bitcast.4, s32[8]{0:T(128)} %gown_hbm.1, f32[8,128]{1,0:T(8,128)} %bitcast.5, s32[8]{0:T(128)} %mown_hbm.1, ...), custom_call_target="tpu_custom_call" | custom-call | tf_op jit(solution)/shard_map/step/pallas_call | solution.py:480
  35.9 2.1 %last.1 = (bf16[8,128,512]{2,1,0:T(8,128)(2,1)}, bf16[128,512]{1,0:T(8,128)(2,1)}) custom-call(bf16[8,128,512]{2,1,0:T(8,128)(2,1)S(1)} %get-tuple-element.9.res, bf16[256,512]{1,0:T(8,128)(2,1)S(1)} %get-tuple-element.10.rin, bf16[128,512]{1,0:T(8,128)(2,1)S(1)} %get-tuple-element.11.mesh, bf16[256,2048]{1,0:T(8,128)(2,1)S(1)} %get-tuple-element.12.hid, ...), custom_call_target="tpu_custom_call" | custom-call | tf_op jit(solution)/shard_map/last/pallas_call | solution.py:536
